TPU v7x, 256 devices: a whole 4x4x8 slice. The times are simulated.
256 devices in a mesh: species: 16 (over y, z_lo, core), tile: 16 (over x, z_hi).
Axes of the slice: x: 4, y: 4, z: 8 (z_hi: 4, z_lo: 2; z = z_hi * 2 + z_lo), core: 2. Of those that a mesh axis runs over, the one named last changes fastest.
Arguments:
- tracers: float32 [256, 16, 128, 128], P('species', None, 'tile'), may hold values from 0.1 to 4
- fluxes: float32 [4, 3, 16, 128, 128], P(None, None, 'species', 'tile'), may hold values from -0.15 to 0.15
- weight_in: bfloat16 [512, 256], replicated, may hold values from -0.375 to 0.375
- weight_out: bfloat16 [256, 512], replicated, may hold values from -0.25 to 0.25
Outputs:
- tracers_out: float32 [256, 16, 128, 128], P('species', None, 'tile')
All inputs are finite; a program needn't handle non-finite values.
Results may differ from a plain program's by a relative error of at most 0.0035.
Values may be sent and summed in bfloat16 or wider, within the bound.
A program may use at most 64 MiB of HBM per device.

v0:
```python
import jax
import jax.numpy as jnp
from jax import lax
from jax.sharding import PartitionSpec as P

STEPS = 4


def extended(cells, sides, width):
    for axis, dim in sides:
        count = lax.axis_size(axis)
        ends = count - 1
        head = lax.slice_in_dim(cells, 0, width, axis=dim)
        tail = lax.slice_in_dim(cells, cells.shape[dim] - width, cells.shape[dim], axis=dim)
        cells = jnp.concatenate(
            [
                lax.ppermute(tail, axis, [(i, (i + 1) % count) for i in range(ends)]),
                cells,
                lax.ppermute(head, axis, [((i + 1) % count, i) for i in range(ends)]),
            ],
            axis=dim,
        )
    return cells


def positive(value):
    return jnp.maximum(value, 0.0)


def negative(value):
    return jnp.minimum(value, 0.0)


def advance(padded_state, padded_x, flux_y, padded_z):
    inner = padded_state[:, 1:-1, 1:-1]
    along_x = padded_state[:, 1:-1]
    face_x = padded_x[:, 1:]
    faces_x = positive(face_x) * along_x[:, :, :-1] + negative(face_x) * along_x[:, :, 1:]
    along_z = padded_state[:, :, 1:-1]
    face_z = padded_z[1:]
    faces_z = positive(face_z) * along_z[:, :-1] + negative(face_z) * along_z[:, 1:]
    faces_y = positive(flux_y) * jnp.roll(inner, 1, 3) + negative(flux_y) * inner
    return (
        inner
        + faces_x[:, :, :-1]
        - faces_x[:, :, 1:]
        + faces_y
        - jnp.roll(faces_y, -1, 3)
        + faces_z[:, :-1]
        - faces_z[:, 1:]
    )


def per_device(tracers, fluxes, weight_in, weight_out):
    spec_loc, depth_all, width_x, width_y = tracers.shape
    tile_at = lax.axis_index("tile")
    grid_shape = (depth_all, width_x, width_y)
    column = tile_at * width_x + lax.broadcasted_iota(jnp.int32, grid_shape, 1)
    level_at = lax.broadcasted_iota(jnp.int32, grid_shape, 0)
    state = tracers
    for interval in range(STEPS):
        gathered = lax.all_gather(fluxes[interval], "species", axis=1, tiled=True)
        flux_x = jnp.where(column == 0, 0.0, gathered[0])
        flux_y = gathered[1]
        flux_z = jnp.where(level_at == 0, 0.0, gathered[2])
        stacked = jnp.concatenate([state, flux_x[None]], 0)
        padded = extended(stacked, (("tile", 2),), 1)
        padded_state = jnp.pad(padded[:spec_loc], ((0, 0), (1, 1), (0, 0), (0, 0)))
        padded_x = padded[spec_loc]
        padded_z = jnp.pad(flux_z, ((1, 1), (0, 0), (0, 0)))
        state = advance(padded_state, padded_x, flux_y, padded_z)
        flattened = state.astype(jnp.bfloat16).reshape(spec_loc, depth_all, width_x * width_y)
        hidden = jax.nn.silu(
            jnp.einsum(
                "hs,szc->hzc",
                weight_in,
                lax.all_to_all(flattened, "species", split_axis=1, concat_axis=0, tiled=True),
                preferred_element_type=jnp.float32,
            )
        ).astype(jnp.bfloat16)
        tendency = (
            0.5 * jnp.einsum("sh,hzc->szc", weight_out, hidden, preferred_element_type=jnp.float32)
        ).astype(jnp.bfloat16)
        returned = lax.all_to_all(tendency, "species", split_axis=0, concat_axis=1, tiled=True)
        state = state + returned.reshape(state.shape).astype(jnp.float32)
    return state


def solution(mesh):
    placed = (P("species", None, "tile", None), P(None, None, "species", "tile", None), P(), P())
    return jax.shard_map(
        per_device,
        mesh=mesh,
        in_specs=placed,
        out_specs=P("species", None, "tile", None),
        check_vma=False,
    )
```

profile of v0, /device:TPU:2, one launch (start us, length us, event | category | flops | bytes accessed | tf_op | source)
XLA Modules:
  0.0 284.3 jit_solution(3213758071041824670)
XLA Ops:
  0.0 0.9 fusion.78
  0.9 21.1 %all-gather = f32[1,3,16,8,128]{4,3,1,0,2:T(8,128)S(1)} all-gather(f32[1,3,1,8,128]{4,3,1,0,2:T(8,128)S(1)} %get-tuple-element.47), channel_id=2, replica_groups=mesh['species'=16,'tile'=16] {'species'}, dimensions={2}, use_global_device_ids=true | all-gather | bytes 208896 | tf_op jit(solution)/shard_map/all_gather | solution.py:62
  21.9 17.0 %all-gather.1 = f32[1,3,16,8,128]{4,3,1,0,2:T(8,128)S(1)} all-gather(f32[1,3,1,8,128]{4,3,1,0,2:T(8,128)S(1)} %get-tuple-element.50), channel_id=3, replica_groups=mesh['species'=16,'tile'=16] {'species'}, dimensions={2}, use_global_device_ids=true | all-gather | bytes 208896 | tf_op jit(solution)/shard_map/all_gather | solution.py:62
  39.0 18.4 %all-gather.2 = f32[1,3,16,8,128]{4,3,1,0,2:T(8,128)S(1)} all-gather(f32[1,3,1,8,128]{4,3,1,0,2:T(8,128)S(1)} %get-tuple-element.49), channel_id=4, replica_groups=mesh['species'=16,'tile'=16] {'species'}, dimensions={2}, use_global_device_ids=true | all-gather | bytes 208896 | tf_op jit(solution)/shard_map/all_gather | solution.py:62
  57.3 17.0 %all-gather.3 = f32[1,3,16,8,128]{4,3,1,0,2:T(8,128)S(1)} all-gather(f32[1,3,1,8,128]{4,3,1,0,2:T(8,128)S(1)} %get-tuple-element.48), channel_id=5, replica_groups=mesh['species'=16,'tile'=16] {'species'}, dimensions={2}, use_global_device_ids=true | all-gather | bytes 208896 | tf_op jit(solution)/shard_map/all_gather | solution.py:62
  74.4 1.6 slice.444
  76.4 0.8 fusion.60
  77.8 7.3 %collective-permute-start.1 = (f32[17,16,1,128]{3,1,2,0:T(8,128)S(1)}, f32[17,16,1,128]{3,1,2,0:T(8,128)S(1)}, u32[]{:S(2)}, u32[]{:S(2)}) collective-permute-start(f32[17,16,1,128]{3,1,2,0:T(8,128)S(1)} %get-tuple-element.20), channel_id=1, source_target_pairs={{1,0},{2,1},{3,2},{4,3},{5,4},{6,5},{7,6},{8,7},{9,8},{10,9},{11,1... | collective-permute-start | bytes 417800 | tf_op jit(solution)/shard_map/ppermute | solution.py:19
  85.1 1.9 collective-permute-start
  87.0 0.7 fusion.53
  87.8 0.7 fusion.62
  88.8 1.5 collective-permute-done.1
  90.3 8.3 %collective-permute-done = f32[17,16,1,128]{3,1,2,0:T(8,128)S(1)} collective-permute-done((f32[17,16,1,128]{3,1,2,0:T(8,128)S(1)}, f32[17,16,1,128]{3,1,2,0:T(8,128)S(1)}, u32[]{:S(2)}, u32[]{:S(2)}) %collective-permute-start) | collective-permute-done | bytes 139296 | tf_op jit(solution)/shard_map/ppermute | solution.py:17
  99.3 0.8 fusion.76
  100.5 13.5 %all_to_all.96 = bf16[16,16,1024]{2,0,1:T(8,128)(2,1)S(1)} all-to-all(bf16[16,16,1024]{2,0,1:T(8,128)(2,1)S(1)} %reshape.116), channel_id=1, replica_groups=mesh['species'=16,'tile'=16] {'species'}, dimensions={1} | all-to-all | bytes 1048576 | tf_op jit(solution)/shard_map/all_to_all | solution.py:77
  114.0 0.9 fusion.28
  115.4 1.1 reduce
  116.7 1.2 reshape.176
  117.9 3.6 %all-to-all-start.1 = ((bf16[16,2,8192]{2,1,0:T(2,128)(2,1)}), bf16[16,2,8192]{2,1,0:T(2,128)(2,1)S(1)}, u32[]{:S(2)}, u32[]{:S(2)}) async-start(bf16[16,2,8192]{2,1,0:T(2,128)(2,1)} %reshape.176), calls=%async_computation.1 | async-start | bytes 1048576 | tf_op jit(solution)/shard_map/all_to_all | solution.py:84
  122.9 9.4 %all-to-all-done.1 = bf16[16,2,8192]{2,1,0:T(2,128)(2,1)S(1)} async-done(((bf16[16,2,8192]{2,1,0:T(2,128)(2,1)}), bf16[16,2,8192]{2,1,0:T(2,128)(2,1)S(1)}, u32[]{:S(2)}, u32[]{:S(2)}) %all-to-all-start.1) | async-done | bytes 524320 | tf_op jit(solution)/shard_map/all_to_all | solution.py:84
  134.1 1.9 collective-permute-start.3
  136.0 4.8 %collective-permute-start.2 = (f32[17,16,1,128]{3,1,2,0:T(8,128)S(1)}, f32[17,16,1,128]{3,1,2,0:T(8,128)S(1)}, u32[]{:S(2)}, u32[]{:S(2)}) collective-permute-start(f32[17,16,1,128]{3,1,2,0:T(8,128)S(1)} %get-tuple-element.17), channel_id=1, source_target_pairs={{0,1},{1,2},{2,3},{3,4},{4,5},{5,6},{6,7},{7,8},{8,9},{9,10},{10,1... | collective-permute-start | bytes 417800 | tf_op jit(solution)/shard_map/ppermute | solution.py:17
  141.6 3.2 %collective-permute-done.3 = f32[17,16,1,128]{3,1,2,0:T(8,128)S(1)} collective-permute-done((f32[17,16,1,128]{3,1,2,0:T(8,128)S(1)}, f32[17,16,1,128]{3,1,2,0:T(8,128)S(1)}, u32[]{:S(2)}, u32[]{:S(2)}) %collective-permute-start.3) | collective-permute-done | bytes 139296 | tf_op jit(solution)/shard_map/ppermute | solution.py:19
  144.7 3.8 %collective-permute-done.2 = f32[17,16,1,128]{3,1,2,0:T(8,128)S(1)} collective-permute-done((f32[17,16,1,128]{3,1,2,0:T(8,128)S(1)}, f32[17,16,1,128]{3,1,2,0:T(8,128)S(1)}, u32[]{:S(2)}, u32[]{:S(2)}) %collective-permute-start.2) | collective-permute-done | bytes 139296 | tf_op jit(solution)/shard_map/ppermute | solution.py:17
  151.0 14.3 %all_to_all.97 = bf16[16,16,1024]{2,0,1:T(8,128)(2,1)S(1)} all-to-all(bf16[16,16,1024]{2,0,1:T(8,128)(2,1)S(1)} %reshape.118), channel_id=1, replica_groups=mesh['species'=16,'tile'=16] {'species'}, dimensions={1} | all-to-all | bytes 1048576 | tf_op jit(solution)/shard_map/all_to_all | solution.py:77
  165.2 0.9 fusion.27
  166.1 1.1 reduce.1
  167.4 1.2 reshape.178
  168.6 3.6 %all-to-all-start.3 = ((bf16[16,2,8192]{2,1,0:T(2,128)(2,1)}), bf16[16,2,8192]{2,1,0:T(2,128)(2,1)S(1)}, u32[]{:S(2)}, u32[]{:S(2)}) async-start(bf16[16,2,8192]{2,1,0:T(2,128)(2,1)} %reshape.178), calls=%async_computation.3 | async-start | bytes 1048576 | tf_op jit(solution)/shard_map/all_to_all | solution.py:84
  173.0 10.0 %all-to-all-done.3 = bf16[16,2,8192]{2,1,0:T(2,128)(2,1)S(1)} async-done(((bf16[16,2,8192]{2,1,0:T(2,128)(2,1)}), bf16[16,2,8192]{2,1,0:T(2,128)(2,1)S(1)}, u32[]{:S(2)}, u32[]{:S(2)}) %all-to-all-start.3) | async-done | bytes 524320 | tf_op jit(solution)/shard_map/all_to_all | solution.py:84
  184.8 1.9 collective-permute-start.5
  186.7 4.8 %collective-permute-start.4 = (f32[17,16,1,128]{3,1,2,0:T(8,128)S(1)}, f32[17,16,1,128]{3,1,2,0:T(8,128)S(1)}, u32[]{:S(2)}, u32[]{:S(2)}) collective-permute-start(f32[17,16,1,128]{3,1,2,0:T(8,128)S(1)} %get-tuple-element.15), channel_id=1, source_target_pairs={{0,1},{1,2},{2,3},{3,4},{4,5},{5,6},{6,7},{7,8},{8,9},{9,10},{10,1... | collective-permute-start | bytes 417800 | tf_op jit(solution)/shard_map/ppermute | solution.py:17
  192.3 1.5 collective-permute-done.5
  193.7 4.3 %collective-permute-done.4 = f32[17,16,1,128]{3,1,2,0:T(8,128)S(1)} collective-permute-done((f32[17,16,1,128]{3,1,2,0:T(8,128)S(1)}, f32[17,16,1,128]{3,1,2,0:T(8,128)S(1)}, u32[]{:S(2)}, u32[]{:S(2)}) %collective-permute-start.4) | collective-permute-done | bytes 139296 | tf_op jit(solution)/shard_map/ppermute | solution.py:17
  199.8 15.5 %all_to_all.98 = bf16[16,16,1024]{2,0,1:T(8,128)(2,1)S(1)} all-to-all(bf16[16,16,1024]{2,0,1:T(8,128)(2,1)S(1)} %reshape.120), channel_id=1, replica_groups=mesh['species'=16,'tile'=16] {'species'}, dimensions={1} | all-to-all | bytes 1048576 | tf_op jit(solution)/shard_map/all_to_all | solution.py:77
  215.4 0.9 fusion.26
  216.3 1.1 reduce.2
  217.6 1.2 reshape.180
  218.7 3.6 %all-to-all-start.5 = ((bf16[16,2,8192]{2,1,0:T(2,128)(2,1)}), bf16[16,2,8192]{2,1,0:T(2,128)(2,1)S(1)}, u32[]{:S(2)}, u32[]{:S(2)}) async-start(bf16[16,2,8192]{2,1,0:T(2,128)(2,1)} %reshape.180), calls=%async_computation.5 | async-start | bytes 1048576 | tf_op jit(solution)/shard_map/all_to_all | solution.py:84
  222.5 10.6 %all-to-all-done.5 = bf16[16,2,8192]{2,1,0:T(2,128)(2,1)S(1)} async-done(((bf16[16,2,8192]{2,1,0:T(2,128)(2,1)}), bf16[16,2,8192]{2,1,0:T(2,128)(2,1)S(1)}, u32[]{:S(2)}, u32[]{:S(2)}) %all-to-all-start.5) | async-done | bytes 524320 | tf_op jit(solution)/shard_map/all_to_all | solution.py:84
  234.9 1.9 collective-permute-start.7
  236.9 5.0 %collective-permute-start.6 = (f32[17,16,1,128]{3,1,2,0:T(8,128)S(1)}, f32[17,16,1,128]{3,1,2,0:T(8,128)S(1)}, u32[]{:S(2)}, u32[]{:S(2)}) collective-permute-start(f32[17,16,1,128]{3,1,2,0:T(8,128)S(1)} %get-tuple-element.13), channel_id=1, source_target_pairs={{0,1},{1,2},{2,3},{3,4},{4,5},{5,6},{6,7},{7,8},{8,9},{9,10},{10,1... | collective-permute-start | bytes 417800 | tf_op jit(solution)/shard_map/ppermute | solution.py:17
  242.9 4.4 %collective-permute-done.6 = f32[17,16,1,128]{3,1,2,0:T(8,128)S(1)} collective-permute-done((f32[17,16,1,128]{3,1,2,0:T(8,128)S(1)}, f32[17,16,1,128]{3,1,2,0:T(8,128)S(1)}, u32[]{:S(2)}, u32[]{:S(2)}) %collective-permute-start.6) | collective-permute-done | bytes 139296 | tf_op jit(solution)/shard_map/ppermute | solution.py:17
  249.1 16.4 %all_to_all.99 = bf16[16,16,1024]{2,0,1:T(8,128)(2,1)S(1)} all-to-all(bf16[16,16,1024]{2,0,1:T(8,128)(2,1)S(1)} %reshape.122), channel_id=1, replica_groups=mesh['species'=16,'tile'=16] {'species'}, dimensions={1} | all-to-all | bytes 1048576 | tf_op jit(solution)/shard_map/all_to_all | solution.py:77
  265.5 0.9 fusion.25
  266.4 1.1 reduce.3
  268.1 13.5 %all_to_all.100 = bf16[16,2,8192]{2,1,0:T(2,128)(2,1)S(1)} all-to-all(bf16[16,2,8192]{2,1,0:T(2,128)(2,1)S(1)} %reshape.182), channel_id=1, replica_groups=mesh['species'=16,'tile'=16] {'species'}, dimensions={0} | all-to-all | bytes 1048576 | tf_op jit(solution)/shard_map/all_to_all | solution.py:84
  283.0 1.3 copy.98
  (132 shorter events, 21.7 us)
Async XLA Ops:
  0.0 114.0 %copy-start = (bf16[256,512]{1,0:T(8,128)(2,1)S(1)}, bf16[256,512]{1,0:T(8,128)(2,1)}, u32[]{:S(2)}) copy-start(bf16[256,512]{1,0:T(8,128)(2,1)} %param.7) | copy-start | bytes 786436
  0.0 75.9 %copy-start.1 = (f32[16,16,8,128]{3,2,1,0:T(8,128)S(1)}, f32[16,16,8,128]{3,2,1,0:T(8,128)}, u32[]{:S(2)}) copy-start(f32[16,16,8,128]{3,2,1,0:T(8,128)} %param.4) | copy-start | bytes 3145732
  77.8 12.5 %collective-permute-start.1 = (f32[17,16,1,128]{3,1,2,0:T(8,128)S(1)}, f32[17,16,1,128]{3,1,2,0:T(8,128)S(1)}, u32[]{:S(2)}, u32[]{:S(2)}) collective-permute-start(f32[17,16,1,128]{3,1,2,0:T(8,128)S(1)} %get-tuple-element.20), channel_id=1, source_target_pairs={{1,0},{2,1},{3,2},{4,3},{5,4},{6,5},{7,6},{8,7},{9,8},{10,9},{11,1... | collective-permute-start | bytes 417800 | tf_op jit(solution)/shard_map/ppermute | solution.py:19
  85.1 13.5 %collective-permute-start = (f32[17,16,1,128]{3,1,2,0:T(8,128)S(1)}, f32[17,16,1,128]{3,1,2,0:T(8,128)S(1)}, u32[]{:S(2)}, u32[]{:S(2)}) collective-permute-start(f32[17,16,1,128]{3,1,2,0:T(8,128)S(1)} %get-tuple-element.19), channel_id=1, source_target_pairs={{0,1},{1,2},{2,3},{3,4},{4,5},{5,6},{6,7},{7,8},{8,9},{9,10},{10,1... | collective-permute-start | bytes 417800 | tf_op jit(solution)/shard_map/ppermute | solution.py:17
  100.1 13.8 %copy-start.13 = (bf16[512,256]{1,0:T(8,128)(2,1)S(1)}, bf16[512,256]{1,0:T(8,128)(2,1)}, u32[]{:S(2)}) copy-start(bf16[512,256]{1,0:T(8,128)(2,1)} %param.6) | copy-start | bytes 786436
  116.7 4.8 %copy-start.12 = (f32[1,16,8,128]{3,2,1,0:T(8,128)S(1)}, f32[1,16,8,128]{3,2,1,0:T(8,128)}, u32[]{:S(2)}) copy-start(f32[1,16,8,128]{3,2,1,0:T(8,128)} %get-tuple-element.56) | copy-start | bytes 196612
  116.7 4.8 %copy-start.7 = (f32[17,8,128]{2,1,0:T(8,128)S(1)}, f32[17,8,128]{2,1,0:T(8,128)}, u32[]{:S(2)}) copy-start(f32[17,8,128]{2,1,0:T(8,128)} %get-tuple-element.59) | copy-start | bytes 208900
  116.7 5.5 %copy-start.6 = (f32[17,8,128]{2,1,0:T(8,128)S(1)}, f32[17,8,128]{2,1,0:T(8,128)}, u32[]{:S(2)}) copy-start(f32[17,8,128]{2,1,0:T(8,128)} %get-tuple-element.60) | copy-start | bytes 208900
  117.9 14.4 %all-to-all-start.1 = ((bf16[16,2,8192]{2,1,0:T(2,128)(2,1)}), bf16[16,2,8192]{2,1,0:T(2,128)(2,1)S(1)}, u32[]{:S(2)}, u32[]{:S(2)}) async-start(bf16[16,2,8192]{2,1,0:T(2,128)(2,1)} %reshape.176), calls=%async_computation.1 | async-start | bytes 1048576 | tf_op jit(solution)/shard_map/all_to_all | solution.py:84
  134.1 10.6 %collective-permute-start.3 = (f32[17,16,1,128]{3,1,2,0:T(8,128)S(1)}, f32[17,16,1,128]{3,1,2,0:T(8,128)S(1)}, u32[]{:S(2)}, u32[]{:S(2)}) collective-permute-start(f32[17,16,1,128]{3,1,2,0:T(8,128)S(1)} %get-tuple-element.18), channel_id=1, source_target_pairs={{1,0},{2,1},{3,2},{4,3},{5,4},{6,5},{7,6},{8,7},{9,8},{10,9},{11,1... | collective-permute-start | bytes 417800 | tf_op jit(solution)/shard_map/ppermute | solution.py:19
  136.0 12.5 %collective-permute-start.2 = (f32[17,16,1,128]{3,1,2,0:T(8,128)S(1)}, f32[17,16,1,128]{3,1,2,0:T(8,128)S(1)}, u32[]{:S(2)}, u32[]{:S(2)}) collective-permute-start(f32[17,16,1,128]{3,1,2,0:T(8,128)S(1)} %get-tuple-element.17), channel_id=1, source_target_pairs={{0,1},{1,2},{2,3},{3,4},{4,5},{5,6},{6,7},{7,8},{8,9},{9,10},{10,1... | collective-permute-start | bytes 417800 | tf_op jit(solution)/shard_map/ppermute | solution.py:17
  148.5 0.9 copy-start.2
  148.6 0.9 copy-start.3
  150.6 14.7 %copy-start.14 = (bf16[512,256]{1,0:T(8,128)(2,1)S(1)}, bf16[512,256]{1,0:T(8,128)(2,1)}, u32[]{:S(2)}) copy-start(bf16[512,256]{1,0:T(8,128)(2,1)} %param.6) | copy-start | bytes 786436
  167.2 5.0 %copy-start.11 = (f32[1,16,8,128]{3,2,1,0:T(8,128)S(1)}, f32[1,16,8,128]{3,2,1,0:T(8,128)}, u32[]{:S(2)}) copy-start(f32[1,16,8,128]{3,2,1,0:T(8,128)} %get-tuple-element.57) | copy-start | bytes 196612
  167.2 5.0 %copy-start.8 = (f32[16,8,128]{2,1,0:T(8,128)S(1)}, f32[16,8,128]{2,1,0:T(8,128)}, u32[]{:S(2)}) copy-start(f32[16,8,128]{2,1,0:T(8,128)} %get-tuple-element.51) | copy-start | bytes 196612
  167.2 5.0 %copy-start.9 = (f32[16,8,128]{2,1,0:T(8,128)S(1)}, f32[16,8,128]{2,1,0:T(8,128)}, u32[]{:S(2)}) copy-start(f32[16,8,128]{2,1,0:T(8,128)} %get-tuple-element.53) | copy-start | bytes 196612
  168.6 14.4 %all-to-all-start.3 = ((bf16[16,2,8192]{2,1,0:T(2,128)(2,1)}), bf16[16,2,8192]{2,1,0:T(2,128)(2,1)S(1)}, u32[]{:S(2)}, u32[]{:S(2)}) async-start(bf16[16,2,8192]{2,1,0:T(2,128)(2,1)} %reshape.178), calls=%async_computation.3 | async-start | bytes 1048576 | tf_op jit(solution)/shard_map/all_to_all | solution.py:84
  184.8 9.0 %collective-permute-start.5 = (f32[17,16,1,128]{3,1,2,0:T(8,128)S(1)}, f32[17,16,1,128]{3,1,2,0:T(8,128)S(1)}, u32[]{:S(2)}, u32[]{:S(2)}) collective-permute-start(f32[17,16,1,128]{3,1,2,0:T(8,128)S(1)} %get-tuple-element.16), channel_id=1, source_target_pairs={{1,0},{2,1},{3,2},{4,3},{5,4},{6,5},{7,6},{8,7},{9,8},{10,9},{11,1... | collective-permute-start | bytes 417800 | tf_op jit(solution)/shard_map/ppermute | solution.py:19
  186.7 11.3 %collective-permute-start.4 = (f32[17,16,1,128]{3,1,2,0:T(8,128)S(1)}, f32[17,16,1,128]{3,1,2,0:T(8,128)S(1)}, u32[]{:S(2)}, u32[]{:S(2)}) collective-permute-start(f32[17,16,1,128]{3,1,2,0:T(8,128)S(1)} %get-tuple-element.15), channel_id=1, source_target_pairs={{0,1},{1,2},{2,3},{3,4},{4,5},{5,6},{6,7},{7,8},{8,9},{9,10},{10,1... | collective-permute-start | bytes 417800 | tf_op jit(solution)/shard_map/ppermute | solution.py:17
  199.4 15.9 %copy-start.15 = (bf16[512,256]{1,0:T(8,128)(2,1)S(1)}, bf16[512,256]{1,0:T(8,128)(2,1)}, u32[]{:S(2)}) copy-start(bf16[512,256]{1,0:T(8,128)(2,1)} %param.6) | copy-start | bytes 786436
  217.3 5.0 %copy-start.10 = (f32[1,16,8,128]{3,2,1,0:T(8,128)S(1)}, f32[1,16,8,128]{3,2,1,0:T(8,128)}, u32[]{:S(2)}) copy-start(f32[1,16,8,128]{3,2,1,0:T(8,128)} %get-tuple-element.58) | copy-start | bytes 196612
  217.3 5.0 %copy-start.5 = (f32[17,8,128]{2,1,0:T(8,128)S(1)}, f32[17,8,128]{2,1,0:T(8,128)}, u32[]{:S(2)}) copy-start(f32[17,8,128]{2,1,0:T(8,128)} %get-tuple-element.61) | copy-start | bytes 208900
  217.3 5.0 %copy-start.4 = (f32[17,8,128]{2,1,0:T(8,128)S(1)}, f32[17,8,128]{2,1,0:T(8,128)}, u32[]{:S(2)}) copy-start(f32[17,8,128]{2,1,0:T(8,128)} %get-tuple-element.62) | copy-start | bytes 208900
  218.7 14.4 %all-to-all-start.5 = ((bf16[16,2,8192]{2,1,0:T(2,128)(2,1)}), bf16[16,2,8192]{2,1,0:T(2,128)(2,1)S(1)}, u32[]{:S(2)}, u32[]{:S(2)}) async-start(bf16[16,2,8192]{2,1,0:T(2,128)(2,1)} %reshape.180), calls=%async_computation.5 | async-start | bytes 1048576 | tf_op jit(solution)/shard_map/all_to_all | solution.py:84
  234.9 8.0 %collective-permute-start.7 = (f32[17,16,1,128]{3,1,2,0:T(8,128)S(1)}, f32[17,16,1,128]{3,1,2,0:T(8,128)S(1)}, u32[]{:S(2)}, u32[]{:S(2)}) collective-permute-start(f32[17,16,1,128]{3,1,2,0:T(8,128)S(1)} %get-tuple-element.14), channel_id=1, source_target_pairs={{1,0},{2,1},{3,2},{4,3},{5,4},{6,5},{7,6},{8,7},{9,8},{10,9},{11,1... | collective-permute-start | bytes 417800 | tf_op jit(solution)/shard_map/ppermute | solution.py:19
  236.9 10.4 %collective-permute-start.6 = (f32[17,16,1,128]{3,1,2,0:T(8,128)S(1)}, f32[17,16,1,128]{3,1,2,0:T(8,128)S(1)}, u32[]{:S(2)}, u32[]{:S(2)}) collective-permute-start(f32[17,16,1,128]{3,1,2,0:T(8,128)S(1)} %get-tuple-element.13), channel_id=1, source_target_pairs={{0,1},{1,2},{2,3},{3,4},{4,5},{5,6},{6,7},{7,8},{8,9},{9,10},{10,1... | collective-permute-start | bytes 417800 | tf_op jit(solution)/shard_map/ppermute | solution.py:17
  248.7 16.8 %copy-start.16 = (bf16[512,256]{1,0:T(8,128)(2,1)S(1)}, bf16[512,256]{1,0:T(8,128)(2,1)}, u32[]{:S(2)}) copy-start(bf16[512,256]{1,0:T(8,128)(2,1)} %param.6) | copy-start | bytes 786436
where the time goes:
time: 285 us; the launch traced here: 284 us
  blocking collectives  147 us (52%)
  waiting for transfers between devices  57.1 us (20%)
  starting transfers between devices  40.4 us (14%)
  local copies, waits for them, and re-layouts  18.7 us (7%)
  other arithmetic  17.2 us (6%)
  matrix products  3.48 us (1%)
    all_gather x4, blocking collectives, per_device(): gathered = lax.all_gather(fluxes[interval], 'species', axis=1, tiled=True)  73.5 us
    all_to_all x4, blocking collectives, per_device(): lax.all_to_all(flattened, 'species', split_axis=1, concat_axis=0, tiled=T...  59.7 us
    all_to_all x3, waiting for transfers between devices, per_device(): lax.all_to_all(tendency, 'species', split_axis=0, concat_axis=1, tiled=True)  30 us
    ppermute x4, waiting for transfers between devices, extended(): lax.ppermute(tail, axis, [(i, (i + 1) % count) for i in range(ends)])  20.7 us
    ppermute x4, starting transfers between devices, extended(): lax.ppermute(tail, axis, [(i, (i + 1) % count) for i in range(ends)])  16.6 us
    all_to_all x1, blocking collectives, per_device(): lax.all_to_all(tendency, 'species', split_axis=0, concat_axis=1, tiled=True)  13.5 us
    ppermute x4, starting transfers between devices, extended(): lax.ppermute(head, axis, [((i + 1) % count, i) for i in range(ends)])  13 us
    all_to_all x3, starting transfers between devices, per_device(): lax.all_to_all(tendency, 'species', split_axis=0, concat_axis=1, tiled=True)  10.7 us
  transfers between devices with their start and end apart: 11, of which 11 were waited for; matrix products, arithmetic and copies ran while one was open for 2% of the time, Pallas kernels for 0%

commit v1 on v0

--- a/solution.py
+++ b/solution.py
@@ -59,7 +59,9 @@
     level_at = lax.broadcasted_iota(jnp.int32, grid_shape, 0)
     state = tracers
     for interval in range(STEPS):
-        gathered = lax.all_gather(fluxes[interval], "species", axis=1, tiled=True)
+        block = fluxes[interval]
+        stack = jnp.stack([block] * lax.axis_size("species"))
+        gathered = jnp.concatenate(lax.all_to_all(stack, "species", 0, 0), axis=1)
         flux_x = jnp.where(column == 0, 0.0, gathered[0])
         flux_y = gathered[1]
         flux_z = jnp.where(level_at == 0, 0.0, gathered[2])

time: 285 us -> 257 us (0.902)
  blocking collectives: 147 us -> 109 us
  starting transfers between devices: 40.4 us -> 44.5 us
    all_gather x4 -> x0, blocking collectives: 73.5 us -> none  [per_device(): gathered = lax.all_gather(fluxes[interval], 'species', axis=1, tiled=True)]
    all_to_all x0 -> x3, blocking collectives: none -> 34.4 us  [per_device(): gathered = jnp.concatenate(lax.all_to_all(stack, 'species', 0, 0), axis=1)]
    all_to_all x0 -> x1, starting transfers between devices: none -> 4.18 us  [per_device(): gathered = jnp.concatenate(lax.all_to_all(stack, 'species', 0, 0), axis=1)]
    all_to_all x0 -> x3, local copies, waits for them, and re-layouts: none -> 4.17 us  [per_device(): gathered = jnp.concatenate(lax.all_to_all(stack, 'species', 0, 0), axis=1)]
    unnamed x52 -> x36, local copies, waits for them, and re-layouts: 8.29 us -> 7.65 us
  transfers between devices with their start and end apart: 11 -> 12, of which waited for: 11 -> 12; matrix products, arithmetic and copies ran while one was open for 2% -> 4% of each run, Pallas kernels for 0% -> 0%
where the time goes in v1:
time: 257 us; the launch traced here: 255 us
  blocking collectives  109 us (42%)
  waiting for transfers between devices  57.5 us (22%)
  starting transfers between devices  44.5 us (17%)
  local copies, waits for them, and re-layouts  20.4 us (8%)
  other arithmetic  20 us (8%)
  matrix products  3.49 us (1%)
    all_to_all x4, blocking collectives, per_device(): lax.all_to_all(flattened, 'species', split_axis=1, concat_axis=0, tiled=T...  60.7 us
    all_to_all x3, blocking collectives, per_device(): gathered = jnp.concatenate(lax.all_to_all(stack, 'species', 0, 0), axis=1)  34.4 us
    all_to_all x3, waiting for transfers between devices, per_device(): lax.all_to_all(tendency, 'species', split_axis=0, concat_axis=1, tiled=True)  29.4 us
    ppermute x4, waiting for transfers between devices, extended(): lax.ppermute(tail, axis, [(i, (i + 1) % count) for i in range(ends)])  19.8 us
    ppermute x4, starting transfers between devices, extended(): lax.ppermute(tail, axis, [(i, (i + 1) % count) for i in range(ends)])  16.5 us
    all_to_all x1, blocking collectives, per_device(): lax.all_to_all(tendency, 'species', split_axis=0, concat_axis=1, tiled=True)  13.5 us
    ppermute x4, starting transfers between devices, extended(): lax.ppermute(head, axis, [((i + 1) % count, i) for i in range(ends)])  13.2 us
    all_to_all x3, starting transfers between devices, per_device(): lax.all_to_all(tendency, 'species', split_axis=0, concat_axis=1, tiled=True)  10.7 us
  transfers between devices with their start and end apart: 12, of which 12 were waited for; matrix products, arithmetic and copies ran while one was open for 4% of the time, Pallas kernels for 0%

profile of v1, /device:TPU:2, one launch (start us, length us, event | category | flops | bytes accessed | tf_op | source)
XLA Modules:
  0.0 255.3 jit_solution(14831959644512778129)
XLA Ops:
  0.9 13.2 %all_to_all.116 = f32[16,3,1,8,128]{4,3,2,1,0:T(8,128)} all-to-all(f32[16,3,1,8,128]{4,3,2,1,0:T(8,128)S(1)} %stack.12), channel_id=1, replica_groups=mesh['species'=16,'tile'=16] {'species'}, dimensions={0} | all-to-all | bytes 393216 | tf_op jit(solution)/shard_map/all_to_all | solution.py:64
  14.1 10.6 %all_to_all.117 = f32[16,3,1,8,128]{4,3,2,1,0:T(8,128)} all-to-all(f32[16,3,1,8,128]{4,3,2,1,0:T(8,128)S(1)} %stack.13), channel_id=1, replica_groups=mesh['species'=16,'tile'=16] {'species'}, dimensions={0} | all-to-all | bytes 393216 | tf_op jit(solution)/shard_map/all_to_all | solution.py:64
  24.7 10.6 %all_to_all.118 = f32[16,3,1,8,128]{4,3,2,1,0:T(8,128)} all-to-all(f32[16,3,1,8,128]{4,3,2,1,0:T(8,128)S(1)} %stack.14), channel_id=1, replica_groups=mesh['species'=16,'tile'=16] {'species'}, dimensions={0} | all-to-all | bytes 393216 | tf_op jit(solution)/shard_map/all_to_all | solution.py:64
  36.0 4.2 %all-to-all-start.9 = ((f32[16,3,1,8,128]{4,3,2,1,0:T(8,128)}), f32[16,3,1,8,128]{4,3,2,1,0:T(8,128)}, u32[]{:S(2)}, u32[]{:S(2)}) async-start(f32[16,3,1,8,128]{4,3,2,1,0:T(8,128)} %stack.15), calls=%async_computation.9 | async-start | bytes 393216 | tf_op jit(solution)/shard_map/all_to_all | solution.py:64
  41.8 1.6 copy.94
  43.4 1.6 copy.93
  45.1 2.4 all-to-all-done.9
  47.5 0.9 copy.92
  48.5 1.7 fusion.60
  50.9 7.3 %collective-permute-start.1 = (f32[17,16,1,128]{3,1,2,0:T(8,128)S(1)}, f32[17,16,1,128]{3,1,2,0:T(8,128)S(1)}, u32[]{:S(2)}, u32[]{:S(2)}) collective-permute-start(f32[17,16,1,128]{3,1,2,0:T(8,128)S(1)} %get-tuple-element.20), channel_id=1, source_target_pairs={{1,0},{2,1},{3,2},{4,3},{5,4},{6,5},{7,6},{8,7},{9,8},{10,9},{11,1... | collective-permute-start | bytes 417800 | tf_op jit(solution)/shard_map/ppermute | solution.py:19
  58.1 1.9 collective-permute-start
  60.1 1.0 fusion.53
  61.5 1.1 collective-permute-done.1
  62.6 7.6 %collective-permute-done = f32[17,16,1,128]{3,1,2,0:T(8,128)S(1)} collective-permute-done((f32[17,16,1,128]{3,1,2,0:T(8,128)S(1)}, f32[17,16,1,128]{3,1,2,0:T(8,128)S(1)}, u32[]{:S(2)}, u32[]{:S(2)}) %collective-permute-start) | collective-permute-done | bytes 139296 | tf_op jit(solution)/shard_map/ppermute | solution.py:17
  72.1 14.1 %all_to_all.119 = bf16[16,16,1024]{2,0,1:T(8,128)(2,1)S(1)} all-to-all(bf16[16,16,1024]{2,0,1:T(8,128)(2,1)S(1)} %reshape.265), channel_id=1, replica_groups=mesh['species'=16,'tile'=16] {'species'}, dimensions={1} | all-to-all | bytes 1048576 | tf_op jit(solution)/shard_map/all_to_all | solution.py:79
  86.2 0.9 fusion.28
  87.6 0.9 reduce
  88.8 1.2 reshape.284
  90.0 3.6 %all-to-all-start.2 = ((bf16[16,2,8192]{2,1,0:T(2,128)(2,1)}), bf16[16,2,8192]{2,1,0:T(2,128)(2,1)S(1)}, u32[]{:S(2)}, u32[]{:S(2)}) async-start(bf16[16,2,8192]{2,1,0:T(2,128)(2,1)} %reshape.284), calls=%async_computation.2 | async-start | bytes 1048576 | tf_op jit(solution)/shard_map/all_to_all | solution.py:86
  94.5 9.8 %all-to-all-done.2 = bf16[16,2,8192]{2,1,0:T(2,128)(2,1)S(1)} async-done(((bf16[16,2,8192]{2,1,0:T(2,128)(2,1)}), bf16[16,2,8192]{2,1,0:T(2,128)(2,1)S(1)}, u32[]{:S(2)}, u32[]{:S(2)}) %all-to-all-start.2) | async-done | bytes 524320 | tf_op jit(solution)/shard_map/all_to_all | solution.py:86
  106.2 2.1 collective-permute-start.3
  108.2 4.7 %collective-permute-start.2 = (f32[17,16,1,128]{3,1,2,0:T(8,128)S(1)}, f32[17,16,1,128]{3,1,2,0:T(8,128)S(1)}, u32[]{:S(2)}, u32[]{:S(2)}) collective-permute-start(f32[17,16,1,128]{3,1,2,0:T(8,128)S(1)} %get-tuple-element.17), channel_id=1, source_target_pairs={{0,1},{1,2},{2,3},{3,4},{4,5},{5,6},{6,7},{7,8},{8,9},{9,10},{10,1... | collective-permute-start | bytes 417800 | tf_op jit(solution)/shard_map/ppermute | solution.py:17
  113.7 3.2 %collective-permute-done.3 = f32[17,16,1,128]{3,1,2,0:T(8,128)S(1)} collective-permute-done((f32[17,16,1,128]{3,1,2,0:T(8,128)S(1)}, f32[17,16,1,128]{3,1,2,0:T(8,128)S(1)}, u32[]{:S(2)}, u32[]{:S(2)}) %collective-permute-start.3) | collective-permute-done | bytes 139296 | tf_op jit(solution)/shard_map/ppermute | solution.py:19
  116.9 3.7 %collective-permute-done.2 = f32[17,16,1,128]{3,1,2,0:T(8,128)S(1)} collective-permute-done((f32[17,16,1,128]{3,1,2,0:T(8,128)S(1)}, f32[17,16,1,128]{3,1,2,0:T(8,128)S(1)}, u32[]{:S(2)}, u32[]{:S(2)}) %collective-permute-start.2) | collective-permute-done | bytes 139296 | tf_op jit(solution)/shard_map/ppermute | solution.py:17
  122.4 14.3 %all_to_all.120 = bf16[16,16,1024]{2,0,1:T(8,128)(2,1)S(1)} all-to-all(bf16[16,16,1024]{2,0,1:T(8,128)(2,1)S(1)} %reshape.268), channel_id=1, replica_groups=mesh['species'=16,'tile'=16] {'species'}, dimensions={1} | all-to-all | bytes 1048576 | tf_op jit(solution)/shard_map/all_to_all | solution.py:79
  136.7 0.9 fusion.27
  137.5 0.9 reduce.1
  138.7 1.2 reshape.286
  139.9 3.6 %all-to-all-start.5 = ((bf16[16,2,8192]{2,1,0:T(2,128)(2,1)}), bf16[16,2,8192]{2,1,0:T(2,128)(2,1)S(1)}, u32[]{:S(2)}, u32[]{:S(2)}) async-start(bf16[16,2,8192]{2,1,0:T(2,128)(2,1)} %reshape.286), calls=%async_computation.5 | async-start | bytes 1048576 | tf_op jit(solution)/shard_map/all_to_all | solution.py:86
  144.5 9.8 %all-to-all-done.5 = bf16[16,2,8192]{2,1,0:T(2,128)(2,1)S(1)} async-done(((bf16[16,2,8192]{2,1,0:T(2,128)(2,1)}), bf16[16,2,8192]{2,1,0:T(2,128)(2,1)S(1)}, u32[]{:S(2)}, u32[]{:S(2)}) %all-to-all-start.5) | async-done | bytes 524320 | tf_op jit(solution)/shard_map/all_to_all | solution.py:86
  156.1 1.9 collective-permute-start.5
  158.0 4.8 %collective-permute-start.4 = (f32[17,16,1,128]{3,1,2,0:T(8,128)S(1)}, f32[17,16,1,128]{3,1,2,0:T(8,128)S(1)}, u32[]{:S(2)}, u32[]{:S(2)}) collective-permute-start(f32[17,16,1,128]{3,1,2,0:T(8,128)S(1)} %get-tuple-element.15), channel_id=1, source_target_pairs={{0,1},{1,2},{2,3},{3,4},{4,5},{5,6},{6,7},{7,8},{8,9},{9,10},{10,1... | collective-permute-start | bytes 417800 | tf_op jit(solution)/shard_map/ppermute | solution.py:17
  163.6 1.3 collective-permute-done.5
  164.9 4.5 %collective-permute-done.4 = f32[17,16,1,128]{3,1,2,0:T(8,128)S(1)} collective-permute-done((f32[17,16,1,128]{3,1,2,0:T(8,128)S(1)}, f32[17,16,1,128]{3,1,2,0:T(8,128)S(1)}, u32[]{:S(2)}, u32[]{:S(2)}) %collective-permute-start.4) | collective-permute-done | bytes 139296 | tf_op jit(solution)/shard_map/ppermute | solution.py:17
  171.1 15.5 %all_to_all.121 = bf16[16,16,1024]{2,0,1:T(8,128)(2,1)S(1)} all-to-all(bf16[16,16,1024]{2,0,1:T(8,128)(2,1)S(1)} %reshape.271), channel_id=1, replica_groups=mesh['species'=16,'tile'=16] {'species'}, dimensions={1} | all-to-all | bytes 1048576 | tf_op jit(solution)/shard_map/all_to_all | solution.py:79
  186.7 0.9 fusion.26
  187.6 0.9 reduce.2
  188.7 1.2 reshape.288
  189.9 3.6 %all-to-all-start.8 = ((bf16[16,2,8192]{2,1,0:T(2,128)(2,1)}), bf16[16,2,8192]{2,1,0:T(2,128)(2,1)S(1)}, u32[]{:S(2)}, u32[]{:S(2)}) async-start(bf16[16,2,8192]{2,1,0:T(2,128)(2,1)} %reshape.288), calls=%async_computation.8 | async-start | bytes 1048576 | tf_op jit(solution)/shard_map/all_to_all | solution.py:86
  194.5 9.8 %all-to-all-done.8 = bf16[16,2,8192]{2,1,0:T(2,128)(2,1)S(1)} async-done(((bf16[16,2,8192]{2,1,0:T(2,128)(2,1)}), bf16[16,2,8192]{2,1,0:T(2,128)(2,1)S(1)}, u32[]{:S(2)}, u32[]{:S(2)}) %all-to-all-start.8) | async-done | bytes 524320 | tf_op jit(solution)/shard_map/all_to_all | solution.py:86
  206.1 1.9 collective-permute-start.7
  208.0 5.0 %collective-permute-start.6 = (f32[17,16,1,128]{3,1,2,0:T(8,128)S(1)}, f32[17,16,1,128]{3,1,2,0:T(8,128)S(1)}, u32[]{:S(2)}, u32[]{:S(2)}) collective-permute-start(f32[17,16,1,128]{3,1,2,0:T(8,128)S(1)} %get-tuple-element.13), channel_id=1, source_target_pairs={{0,1},{1,2},{2,3},{3,4},{4,5},{5,6},{6,7},{7,8},{8,9},{9,10},{10,1... | collective-permute-start | bytes 417800 | tf_op jit(solution)/shard_map/ppermute | solution.py:17
  214.1 4.0 %collective-permute-done.6 = f32[17,16,1,128]{3,1,2,0:T(8,128)S(1)} collective-permute-done((f32[17,16,1,128]{3,1,2,0:T(8,128)S(1)}, f32[17,16,1,128]{3,1,2,0:T(8,128)S(1)}, u32[]{:S(2)}, u32[]{:S(2)}) %collective-permute-start.6) | collective-permute-done | bytes 139296 | tf_op jit(solution)/shard_map/ppermute | solution.py:17
  219.9 16.8 %all_to_all.122 = bf16[16,16,1024]{2,0,1:T(8,128)(2,1)S(1)} all-to-all(bf16[16,16,1024]{2,0,1:T(8,128)(2,1)S(1)} %reshape.274), channel_id=1, replica_groups=mesh['species'=16,'tile'=16] {'species'}, dimensions={1} | all-to-all | bytes 1048576 | tf_op jit(solution)/shard_map/all_to_all | solution.py:79
  236.7 0.9 fusion.25
  237.6 0.9 reduce.3
  239.1 13.5 %all_to_all.123 = bf16[16,2,8192]{2,1,0:T(2,128)(2,1)S(1)} all-to-all(bf16[16,2,8192]{2,1,0:T(2,128)(2,1)S(1)} %reshape.290), channel_id=1, replica_groups=mesh['species'=16,'tile'=16] {'species'}, dimensions={0} | all-to-all | bytes 1048576 | tf_op jit(solution)/shard_map/all_to_all | solution.py:86
  254.0 1.3 copy.67
  (124 shorter events, 25.2 us)
Async XLA Ops:
  0.0 86.2 %copy-start = (bf16[256,512]{1,0:T(8,128)(2,1)S(1)}, bf16[256,512]{1,0:T(8,128)(2,1)}, u32[]{:S(2)}) copy-start(bf16[256,512]{1,0:T(8,128)(2,1)} %param.7) | copy-start | bytes 786436
  0.0 40.2 %copy-start.1 = (f32[16,16,8,128]{3,2,1,0:T(8,128)S(1)}, f32[16,16,8,128]{3,2,1,0:T(8,128)}, u32[]{:S(2)}) copy-start(f32[16,16,8,128]{3,2,1,0:T(8,128)} %param.4) | copy-start | bytes 3145732
  36.0 11.5 %all-to-all-start.9 = ((f32[16,3,1,8,128]{4,3,2,1,0:T(8,128)}), f32[16,3,1,8,128]{4,3,2,1,0:T(8,128)}, u32[]{:S(2)}, u32[]{:S(2)}) async-start(f32[16,3,1,8,128]{4,3,2,1,0:T(8,128)} %stack.15), calls=%async_computation.9 | async-start | bytes 393216 | tf_op jit(solution)/shard_map/all_to_all | solution.py:64
  48.4 11.6 %copy-start.2 = (f32[16,3,1,8,128]{4,3,0,2,1:T(8,128)}, f32[16,3,1,8,128]{4,3,0,2,1:T(8,128)S(1)}, u32[]{:S(2)}) copy-start(f32[16,3,1,8,128]{4,3,0,2,1:T(8,128)S(1)} %copy.92) | copy-start | bytes 589828
  50.9 11.7 %collective-permute-start.1 = (f32[17,16,1,128]{3,1,2,0:T(8,128)S(1)}, f32[17,16,1,128]{3,1,2,0:T(8,128)S(1)}, u32[]{:S(2)}, u32[]{:S(2)}) collective-permute-start(f32[17,16,1,128]{3,1,2,0:T(8,128)S(1)} %get-tuple-element.20), channel_id=1, source_target_pairs={{1,0},{2,1},{3,2},{4,3},{5,4},{6,5},{7,6},{8,7},{9,8},{10,9},{11,1... | collective-permute-start | bytes 417800 | tf_op jit(solution)/shard_map/ppermute | solution.py:19
  58.1 12.1 %collective-permute-start = (f32[17,16,1,128]{3,1,2,0:T(8,128)S(1)}, f32[17,16,1,128]{3,1,2,0:T(8,128)S(1)}, u32[]{:S(2)}, u32[]{:S(2)}) collective-permute-start(f32[17,16,1,128]{3,1,2,0:T(8,128)S(1)} %get-tuple-element.19), channel_id=1, source_target_pairs={{0,1},{1,2},{2,3},{3,4},{4,5},{5,6},{6,7},{7,8},{8,9},{9,10},{10,1... | collective-permute-start | bytes 417800 | tf_op jit(solution)/shard_map/ppermute | solution.py:17
  71.7 14.5 %copy-start.6 = (bf16[512,256]{1,0:T(8,128)(2,1)S(1)}, bf16[512,256]{1,0:T(8,128)(2,1)}, u32[]{:S(2)}) copy-start(bf16[512,256]{1,0:T(8,128)(2,1)} %param.6) | copy-start | bytes 786436
  88.6 5.0 %copy-start.5 = (f32[1,16,8,128]{3,2,1,0:T(8,128)S(1)}, f32[1,16,8,128]{3,2,1,0:T(8,128)}, u32[]{:S(2)}) copy-start(f32[1,16,8,128]{3,2,1,0:T(8,128)} %get-tuple-element.56) | copy-start | bytes 196612
  90.0 14.4 %all-to-all-start.2 = ((bf16[16,2,8192]{2,1,0:T(2,128)(2,1)}), bf16[16,2,8192]{2,1,0:T(2,128)(2,1)S(1)}, u32[]{:S(2)}, u32[]{:S(2)}) async-start(bf16[16,2,8192]{2,1,0:T(2,128)(2,1)} %reshape.284), calls=%async_computation.2 | async-start | bytes 1048576 | tf_op jit(solution)/shard_map/all_to_all | solution.py:86
  106.2 10.7 %collective-permute-start.3 = (f32[17,16,1,128]{3,1,2,0:T(8,128)S(1)}, f32[17,16,1,128]{3,1,2,0:T(8,128)S(1)}, u32[]{:S(2)}, u32[]{:S(2)}) collective-permute-start(f32[17,16,1,128]{3,1,2,0:T(8,128)S(1)} %get-tuple-element.18), channel_id=1, source_target_pairs={{1,0},{2,1},{3,2},{4,3},{5,4},{6,5},{7,6},{8,7},{9,8},{10,9},{11,1... | collective-permute-start | bytes 417800 | tf_op jit(solution)/shard_map/ppermute | solution.py:19
  108.2 12.4 %collective-permute-start.2 = (f32[17,16,1,128]{3,1,2,0:T(8,128)S(1)}, f32[17,16,1,128]{3,1,2,0:T(8,128)S(1)}, u32[]{:S(2)}, u32[]{:S(2)}) collective-permute-start(f32[17,16,1,128]{3,1,2,0:T(8,128)S(1)} %get-tuple-element.17), channel_id=1, source_target_pairs={{0,1},{1,2},{2,3},{3,4},{4,5},{5,6},{6,7},{7,8},{8,9},{9,10},{10,1... | collective-permute-start | bytes 417800 | tf_op jit(solution)/shard_map/ppermute | solution.py:17
  122.0 14.7 %copy-start.7 = (bf16[512,256]{1,0:T(8,128)(2,1)S(1)}, bf16[512,256]{1,0:T(8,128)(2,1)}, u32[]{:S(2)}) copy-start(bf16[512,256]{1,0:T(8,128)(2,1)} %param.6) | copy-start | bytes 786436
  138.5 5.0 %copy-start.4 = (f32[1,16,8,128]{3,2,1,0:T(8,128)S(1)}, f32[1,16,8,128]{3,2,1,0:T(8,128)}, u32[]{:S(2)}) copy-start(f32[1,16,8,128]{3,2,1,0:T(8,128)} %get-tuple-element.57) | copy-start | bytes 196612
  139.9 14.4 %all-to-all-start.5 = ((bf16[16,2,8192]{2,1,0:T(2,128)(2,1)}), bf16[16,2,8192]{2,1,0:T(2,128)(2,1)S(1)}, u32[]{:S(2)}, u32[]{:S(2)}) async-start(bf16[16,2,8192]{2,1,0:T(2,128)(2,1)} %reshape.286), calls=%async_computation.5 | async-start | bytes 1048576 | tf_op jit(solution)/shard_map/all_to_all | solution.py:86
  156.1 8.8 %collective-permute-start.5 = (f32[17,16,1,128]{3,1,2,0:T(8,128)S(1)}, f32[17,16,1,128]{3,1,2,0:T(8,128)S(1)}, u32[]{:S(2)}, u32[]{:S(2)}) collective-permute-start(f32[17,16,1,128]{3,1,2,0:T(8,128)S(1)} %get-tuple-element.16), channel_id=1, source_target_pairs={{1,0},{2,1},{3,2},{4,3},{5,4},{6,5},{7,6},{8,7},{9,8},{10,9},{11,1... | collective-permute-start | bytes 417800 | tf_op jit(solution)/shard_map/ppermute | solution.py:19
  158.0 11.3 %collective-permute-start.4 = (f32[17,16,1,128]{3,1,2,0:T(8,128)S(1)}, f32[17,16,1,128]{3,1,2,0:T(8,128)S(1)}, u32[]{:S(2)}, u32[]{:S(2)}) collective-permute-start(f32[17,16,1,128]{3,1,2,0:T(8,128)S(1)} %get-tuple-element.15), channel_id=1, source_target_pairs={{0,1},{1,2},{2,3},{3,4},{4,5},{5,6},{6,7},{7,8},{8,9},{9,10},{10,1... | collective-permute-start | bytes 417800 | tf_op jit(solution)/shard_map/ppermute | solution.py:17
  170.8 15.9 %copy-start.8 = (bf16[512,256]{1,0:T(8,128)(2,1)S(1)}, bf16[512,256]{1,0:T(8,128)(2,1)}, u32[]{:S(2)}) copy-start(bf16[512,256]{1,0:T(8,128)(2,1)} %param.6) | copy-start | bytes 786436
  188.5 5.0 %copy-start.3 = (f32[1,16,8,128]{3,2,1,0:T(8,128)S(1)}, f32[1,16,8,128]{3,2,1,0:T(8,128)}, u32[]{:S(2)}) copy-start(f32[1,16,8,128]{3,2,1,0:T(8,128)} %get-tuple-element.58) | copy-start | bytes 196612
  189.9 14.4 %all-to-all-start.8 = ((bf16[16,2,8192]{2,1,0:T(2,128)(2,1)}), bf16[16,2,8192]{2,1,0:T(2,128)(2,1)S(1)}, u32[]{:S(2)}, u32[]{:S(2)}) async-start(bf16[16,2,8192]{2,1,0:T(2,128)(2,1)} %reshape.288), calls=%async_computation.8 | async-start | bytes 1048576 | tf_op jit(solution)/shard_map/all_to_all | solution.py:86
  206.1 8.0 %collective-permute-start.7 = (f32[17,16,1,128]{3,1,2,0:T(8,128)S(1)}, f32[17,16,1,128]{3,1,2,0:T(8,128)S(1)}, u32[]{:S(2)}, u32[]{:S(2)}) collective-permute-start(f32[17,16,1,128]{3,1,2,0:T(8,128)S(1)} %get-tuple-element.14), channel_id=1, source_target_pairs={{1,0},{2,1},{3,2},{4,3},{5,4},{6,5},{7,6},{8,7},{9,8},{10,9},{11,1... | collective-permute-start | bytes 417800 | tf_op jit(solution)/shard_map/ppermute | solution.py:19
  208.0 10.1 %collective-permute-start.6 = (f32[17,16,1,128]{3,1,2,0:T(8,128)S(1)}, f32[17,16,1,128]{3,1,2,0:T(8,128)S(1)}, u32[]{:S(2)}, u32[]{:S(2)}) collective-permute-start(f32[17,16,1,128]{3,1,2,0:T(8,128)S(1)} %get-tuple-element.13), channel_id=1, source_target_pairs={{0,1},{1,2},{2,3},{3,4},{4,5},{5,6},{6,7},{7,8},{8,9},{9,10},{10,1... | collective-permute-start | bytes 417800 | tf_op jit(solution)/shard_map/ppermute | solution.py:17
